TPU v7x, 32 devices: a whole 2x2x4 slice. The times are simulated.
32 devices in a mesh: parts: 1, rows: 8 (over z, y), branch: 2 (over core), head: 2 (over x).
Axes of the slice: x: 2, y: 2, z: 4, core: 2. Of those that a mesh axis runs over, the one named last changes fastest.
Arguments:
- lineup_state: bfloat16 [32, 128, 256], P(('parts', 'rows', 'branch')), may hold values from -12 to 12
- pairwise: bfloat16 [128, 128, 128], P(('parts', 'rows', 'branch')), may hold values from -12 to 12
- aligned_residue_bounds: int32 [32, 2], P('parts'), may hold values from 0 to 128, as said below
- residue_valid_mask: int32 [128], P('parts'), may hold values from 0 to 1, as said below
- coupling_offset_weight_map: bfloat16 [128, 8], P(None, 'head'), may hold values from -0.5 to 0.5
- triangle_bias_matrix: bfloat16 [128, 4], P(None, 'head'), may hold values from -0.5 to 0.5
- alignment_projection_matrix: bfloat16 [4, 256, 256], P(None, None, 'head'), may hold values from -1 to 1
- lineup_readout_weight: bfloat16 [256, 256], replicated, may hold values from -4 to 4
- feedfwd_entry_weight: bfloat16 [256, 1024], P(None, 'head'), may hold values from -0.375 to 0.375
- feedfwd_exit_weight: bfloat16 [1024, 256], P('head'), may hold values from -0.1875 to 0.1875
- pair_projection_matrix: bfloat16 [4, 128, 128], P(None, None, 'head'), may hold values from -2 to 2
- pair_output_matrix: bfloat16 [128, 128], P(None, 'head'), may hold values from -6 to 6
- left_right_maps: bfloat16 [2, 256, 32], replicated, may hold values from -0.375 to 0.375
- outer_product_output_matrix: bfloat16 [1024, 128], P(None, 'head'), may hold values from -1.5 to 1.5
Outputs:
- refreshed_lineup_state: bfloat16 [32, 128, 256], P(('parts', 'rows', 'branch'), None, 'head')
- pairwise_out: bfloat16 [128, 128, 128], P(('parts', 'rows', 'branch'), None, 'head')
Inputs may be any that keep to these rules, and one draw needn't show every extreme that they name: `aligned_residue_bounds`: each row holds a start below its end; row 0 covers all 128 residues; every span covers a quarter of the 128 residues or more and starts in the first half. `residue_valid_mask`: 1 on a prefix that holds at least half of the 128 residues, 0 after it; the last residue is always 0.
All inputs are finite; a program needn't handle non-finite values.
Results may differ from a plain program's by a relative error of at most 0.011.
Values may be sent and summed in bfloat16 or wider, within the bound.
No kernel may reach another device: no remote copies, remote signals or barrier semaphores. Data moves between devices by JAX's collectives and lax.ppermute only.
A program may use at most 64 MiB of HBM per device.

v0:
```python
import math
import jax
import jax.numpy as jnp
from jax import lax
from jax.sharding import PartitionSpec as P

PER_FOCUS_DIM = 32


def layer_normalize(values):
    values = values.astype(jnp.float32)
    center = values - jnp.mean(values, -1, keepdims=True)
    spread = jnp.mean(center * center, -1, keepdims=True)
    return center * lax.rsqrt(spread + 1e-05)


def soft_weights(attention_scores):
    row_max = jnp.max(attention_scores, -1, keepdims=True)
    shifted = jnp.exp(attention_scores - row_max)
    return (shifted / jnp.sum(shifted, -1, keepdims=True)).astype(jnp.bfloat16)


def span_mask(aligned_residue_bounds, length_value):
    places = jnp.arange(length_value, dtype=jnp.int32)
    inside = (places[None, :] >= aligned_residue_bounds[:, 0:1]) & (
        places[None, :] < aligned_residue_bounds[:, 1:2]
    )
    return inside.astype(jnp.float32)


def local(
    lineup_state,
    pairwise,
    aligned_residue_bounds,
    residue_valid_mask,
    coupling_offset_weight_map,
    triangle_bias_matrix,
    alignment_projection_matrix,
    lineup_readout_weight,
    feedfwd_entry_weight,
    feedfwd_exit_weight,
    pair_projection_matrix,
    pair_output_matrix,
    left_right_maps,
    outer_product_output_matrix,
):
    sequence_shard_count = lineup_state.shape[0]
    length_value = lineup_state.shape[1]
    residue_shard_count = pairwise.shape[0]
    alignment_heads_sharded = coupling_offset_weight_map.shape[1]
    pairwise_heads_sharded = triangle_bias_matrix.shape[1]
    inv_scale = 1.0 / math.sqrt(PER_FOCUS_DIM)
    row_place = lax.axis_index(("rows", "branch"))
    head_location = lax.axis_index("head")
    seq_start = row_place * sequence_shard_count
    row_start = row_place * residue_shard_count
    mask_full = span_mask(aligned_residue_bounds, length_value)
    mask_own = lax.dynamic_slice_in_dim(mask_full, seq_start, sequence_shard_count, 0)
    key_valid = residue_valid_mask > 0
    alignment_normed = layer_normalize(lineup_state).astype(jnp.bfloat16)
    pair_normed = layer_normalize(pairwise).astype(jnp.bfloat16)
    bias_matrix = jnp.concatenate([coupling_offset_weight_map, triangle_bias_matrix], axis=1)
    bias_local = jnp.einsum(
        "tue,el->ltu", pair_normed, bias_matrix, preferred_element_type=jnp.float32
    ).astype(jnp.bfloat16)
    lineup_mapped = jnp.einsum(
        "tvf,xfp->xtvp",
        alignment_normed,
        alignment_projection_matrix,
        preferred_element_type=jnp.float32,
    )
    lineup_probe_lookup_content = (
        lineup_mapped[:3]
        .astype(jnp.bfloat16)
        .reshape(3, sequence_shard_count, length_value, alignment_heads_sharded, PER_FOCUS_DIM)
    )
    alignment_gate = jax.nn.sigmoid(lineup_mapped[3])
    pair_proj = jnp.einsum(
        "ijc,gcd->gijd", pair_normed, pair_projection_matrix, preferred_element_type=jnp.float32
    )
    pair_qkv = (
        pair_proj[:3]
        .astype(jnp.bfloat16)
        .reshape(3, residue_shard_count, length_value, pairwise_heads_sharded, PER_FOCUS_DIM)
    )
    pair_gate = jax.nn.sigmoid(pair_proj[3])
    bias_portion = lax.all_gather(bias_local, ("rows", "branch"), axis=1, tiled=True)
    row_total_count = bias_portion.shape[1]
    alignment_query = lineup_probe_lookup_content[0]
    attention_scores = (
        jnp.einsum(
            "xtza,xfza->xztf",
            alignment_query,
            lineup_probe_lookup_content[1],
            preferred_element_type=jnp.float32,
        )
        * inv_scale
    )
    attention_scores = (
        attention_scores + bias_portion[:alignment_heads_sharded].astype(jnp.float32)[None]
    )
    attention_scores = jnp.where(mask_own[:, None, None, :] > 0, attention_scores, -1000000000.0)
    softmax_shares = soft_weights(attention_scores)
    alignment_portion = jnp.einsum(
        "fxkc,fcxz->fkxz",
        softmax_shares,
        lineup_probe_lookup_content[2],
        preferred_element_type=jnp.float32,
    )
    alignment_portion = alignment_portion.reshape(
        sequence_shard_count, row_total_count, alignment_heads_sharded * PER_FOCUS_DIM
    )
    alignment_portion = (alignment_portion * alignment_gate).astype(jnp.bfloat16)
    pair_query = pair_qkv[0]
    triangle_scores = (
        jnp.einsum("ijhd,ikhd->ihjk", pair_query, pair_qkv[1], preferred_element_type=jnp.float32)
        * inv_scale
    )
    triangle_scores = (
        triangle_scores + bias_portion[alignment_heads_sharded:].astype(jnp.float32)[None]
    )
    triangle_scores = jnp.where(key_valid[None, None, None, :], triangle_scores, -1000000000.0)
    tri_weights = soft_weights(triangle_scores)
    pair_part = jnp.einsum(
        "ihjk,ikhd->ijhd", tri_weights, pair_qkv[2], preferred_element_type=jnp.float32
    )
    pair_part = pair_part.reshape(
        residue_shard_count, row_total_count, pairwise_heads_sharded * PER_FOCUS_DIM
    )
    pair_part = (pair_part * pair_gate).astype(jnp.bfloat16)
    alignment_flattened = jnp.transpose(alignment_portion, (1, 0, 2)).reshape(
        row_total_count, sequence_shard_count * alignment_heads_sharded * PER_FOCUS_DIM
    )
    pair_flattened = jnp.transpose(pair_part, (1, 0, 2)).reshape(
        row_total_count, residue_shard_count * pairwise_heads_sharded * PER_FOCUS_DIM
    )
    attention_result = jnp.concatenate([alignment_flattened, pair_flattened], axis=1)
    alignment_width = sequence_shard_count * alignment_heads_sharded * PER_FOCUS_DIM
    alignment_local = jnp.transpose(
        attention_result[:, :alignment_width].reshape(
            length_value, sequence_shard_count, alignment_heads_sharded * PER_FOCUS_DIM
        ),
        (1, 0, 2),
    )
    pair_local = jnp.transpose(
        attention_result[:, alignment_width:].reshape(
            length_value, residue_shard_count, pairwise_heads_sharded * PER_FOCUS_DIM
        ),
        (1, 0, 2),
    )
    lineup_focus_split, pairwise_heads = (
        lax.all_gather(alignment_local, "head", axis=2, tiled=True),
        lax.all_gather(pair_local, "head", axis=2, tiled=True),
    )
    outer_factors = jnp.einsum(
        "juf,bfn->bjun", alignment_normed, left_right_maps, preferred_element_type=jnp.float32
    )
    outer_factors = (outer_factors * mask_own[None, :, :, None]).astype(jnp.bfloat16)
    factor_rows = lax.all_to_all(
        outer_factors[0], ("rows", "branch"), split_axis=1, concat_axis=0, tiled=True
    )
    col_factors = lax.all_gather(outer_factors[1], ("rows", "branch"), axis=0, tiled=True)
    mask_rows = lax.dynamic_slice_in_dim(mask_full, row_start, residue_shard_count, 1)
    pair_count = jnp.dot(mask_rows.T, mask_full, precision=lax.Precision.HIGHEST)
    col_block = math.gcd(length_value, 128)

    def outer_block(col_start):
        block_cols = lax.dynamic_slice_in_dim(col_factors, col_start, col_block, 1)
        outer_sum = lax.dot_general(
            factor_rows, block_cols, (((0,), (0,)), ((), ())), preferred_element_type=jnp.float32
        )
        counts = lax.dynamic_slice_in_dim(pair_count, col_start, col_block, 1)
        outer_mean = (outer_sum / counts[:, None, :, None]).astype(jnp.bfloat16)
        outer_mean = jnp.transpose(outer_mean, (0, 2, 1, 3)).reshape(
            residue_shard_count * col_block, -1
        )
        return jnp.dot(
            outer_mean, outer_product_output_matrix, preferred_element_type=jnp.float32
        ).reshape(residue_shard_count, col_block, -1)

    starts = jnp.arange(length_value // col_block, dtype=jnp.int32) * col_block
    opm_blocks = lax.map(outer_block, starts)
    opm_update = jnp.transpose(opm_blocks, (1, 0, 2, 3)).reshape(
        residue_shard_count, length_value, -1
    )
    width_z = pair_output_matrix.shape[1]
    tri_update = jnp.dot(
        pairwise_heads.reshape(residue_shard_count * length_value, -1),
        pair_output_matrix,
        preferred_element_type=jnp.float32,
    ).reshape(residue_shard_count, length_value, width_z)
    pair_own = lax.dynamic_slice_in_dim(pairwise, head_location * width_z, width_z, 2).astype(
        jnp.float32
    )
    pairwise_out = (pair_own + tri_update + opm_update).astype(jnp.bfloat16)
    channels = lineup_state.shape[2]
    lineup_blended = lineup_state.astype(jnp.float32) + jnp.dot(
        lineup_focus_split.reshape(sequence_shard_count * length_value, -1),
        lineup_readout_weight,
        preferred_element_type=jnp.float32,
    ).reshape(sequence_shard_count, length_value, channels)
    feedfwd_standardized = layer_normalize(lineup_blended).astype(jnp.bfloat16)
    head_count = lax.axis_size("head")
    hidden = jax.nn.relu(
        jnp.einsum(
            "src,cf->srf",
            feedfwd_standardized,
            feedfwd_entry_weight,
            preferred_element_type=jnp.float32,
        )
    ).astype(jnp.bfloat16)
    partial_value = jnp.einsum(
        "srf,fc->src", hidden, feedfwd_exit_weight, preferred_element_type=jnp.float32
    )
    summed_result = lax.psum_scatter(
        partial_value.astype(jnp.bfloat16), "head", scatter_dimension=2, tiled=True
    ).astype(jnp.float32)
    alignment_channel_width = channels // head_count
    alignment_owned = lax.dynamic_slice_in_dim(
        lineup_blended, head_location * alignment_channel_width, alignment_channel_width, 2
    )
    refreshed_lineup_state = (alignment_owned + summed_result).astype(jnp.bfloat16)
    return (refreshed_lineup_state, pairwise_out)


def solution(mesh):
    in_specs = (
        P(("parts", "rows", "branch"), None, None),
        P(("parts", "rows", "branch"), None, None),
        P("parts", None),
        P("parts"),
        P(None, "head"),
        P(None, "head"),
        P(None, None, "head"),
        P(),
        P(None, "head"),
        P("head", None),
        P(None, None, "head"),
        P(None, "head"),
        P(),
        P(None, "head"),
    )
    out_specs = (
        P(("parts", "rows", "branch"), None, "head"),
        P(("parts", "rows", "branch"), None, "head"),
    )
    return jax.shard_map(local, mesh=mesh, in_specs=in_specs, out_specs=out_specs, check_vma=False)
```

profile of v0, /device:TPU:0, one launch (start us, length us, event | category | flops | bytes accessed | tf_op | source)
XLA Modules:
  0.0 93.5 jit_solution(9554350493809274063)
XLA Ops:
  7.2 1.1 %convert_reduce_fusion.1 = f32[2,128]{1,0:T(2,128)S(1)} fusion(bf16[2,128,256]{2,1,0:T(8,128)(2,1)} %param.14), kind=kLoop, calls=%fused_computation.38 | loop fusion | flops 130816 | bytes 132096 | tf_op jit(solution)/shard_map/reduce_sum | solution.py:12
  8.3 1.1 %fusion.24 = f32[2,128]{1,0:T(2,128)S(1)} fusion(bf16[2,128,256]{2,1,0:T(8,128)(2,1)} %param.14, f32[2,128]{1,0:T(2,128)S(1)} %broadcast_multiply_fusion.2), kind=kLoop, calls=%fused_computation.41 | loop fusion | flops 261888 | bytes 133120 | tf_op jit(solution)/shard_map/reduce_sum | solution.py:13
  9.4 0.8 slice_bitcast_fusion.2
  10.2 1.2 %fusion.16 = bf16[2,2,128,32]{2,3,0,1:T(8,128)(2,1)S(1)} fusion(bf16[2,128,256]{2,1,0:T(8,128)(2,1)} %param.14, f32[2,128]{1,0:T(2,128)S(1)} %add_rsqrt_fusion.2, f32[2,128]{1,0:T(2,128)S(1)} %broadcast_multiply_fusion.2, bf16[2,256,32]{1,2,0:T(8,128)(2,1)} %param.26, f32[2,128]{1,0:T(2,128)S(1)} %get-tuple-element.28), kind=kOutput, calls=%fused_computation.26 | convolution fusion | flops 8683520 | bytes 199680 | tf_op jit(solution)/shard_map/juf,bfn->bjun/dot_general | solution.py:155
  11.6 0.7 reshape.117
  12.3 7.4 %all-to-all-start = ((bf16[16,2,256]{2,1,0:T(2,128)(2,1)}), bf16[16,2,256]{2,1,0:T(2,128)(2,1)S(1)}, u32[]{:S(2)}, u32[]{:S(2)}) async-start(bf16[16,2,256]{2,1,0:T(2,128)(2,1)} %reshape.117), calls=%async_computation | async-start | bytes 32768 | tf_op jit(solution)/shard_map/all_to_all | solution.py:159
  19.7 1.1 %convert_reduce_fusion = f32[8,128]{1,0:T(8,128)S(1)} fusion(bf16[8,128,128]{2,1,0:T(8,128)(2,1)} %param.15), kind=kLoop, calls=%fused_computation.30 | loop fusion | flops 261120 | bytes 266240 | tf_op jit(solution)/shard_map/reduce_sum | solution.py:12
  20.9 1.3 %fusion.19 = f32[8,128]{1,0:T(8,128)S(1)} fusion(bf16[8,128,128]{2,1,0:T(8,128)(2,1)} %param.15, f32[8,128]{1,0:T(8,128)S(1)} %broadcast_multiply_fusion), kind=kLoop, calls=%fused_computation.33 | loop fusion | flops 523264 | bytes 270336 | tf_op jit(solution)/shard_map/reduce_sum | solution.py:13
  22.2 1.4 %convolution_convert_fusion = bf16[6,8,128]{2,0,1:T(8,128)(2,1)S(1)} fusion(bf16[8,128,128]{2,1,0:T(8,128)(2,1)} %param.15, f32[8,128]{1,0:T(8,128)S(1)} %add_rsqrt_fusion, f32[8,128]{1,0:T(8,128)S(1)} %broadcast_multiply_fusion, bf16[128,2]{0,1:T(2,128)(2,1)} %param.19, bf16[128,4]{0,1:T(4,128)(2,1)} %param.18), kind=kOutput, calls=%fused_computation.27 | convolution fusion | flops 2106368 | bytes 284160 | tf_op jit(solution)/shard_map/tue,el->ltu/dot_general | solution.py:63
  23.6 22.2 %all_gather.12 = bf16[6,128,128]{2,1,0:T(8,128)(2,1)S(1)} all-gather(bf16[6,8,128]{2,1,0:T(8,128)(2,1)S(1)} %copy.39), channel_id=1, replica_groups=mesh['parts'=1,'rows'=8,'branch'=2,'head'=2] {'rows','branch'}, dimensions={1}, use_global_device_ids=true | all-gather | bytes 208896 | tf_op jit(solution)/shard_map/all_gather | solution.py:87
  46.1 0.4 fusion.78
  46.5 0.4 fusion.79
  46.9 0.3 fusion.10
  47.2 0.2 fusion.40
  47.5 5.1 %all_gather.13 = bf16[2,128,256]{1,2,0:T(8,128)(2,1)S(1)} all-gather(bf16[2,128,128]{1,2,0:T(8,128)(2,1)S(1)} %fusion.55), channel_id=1, replica_groups=mesh['parts'=1,'rows'=8,'branch'=2,'head'=2] {'head'}, dimensions={2}, use_global_device_ids=true | all-gather | bytes 196608 | tf_op jit(solution)/shard_map/all_gather | solution.py:152
  52.6 0.3 fusion.80
  53.0 0.2 multiply_reduce_fusion
  53.2 0.4 fusion.14
  53.7 0.7 copy.76
  54.6 0.9 fusion.81
  55.5 0.6 fusion.82
  56.1 0.4 fusion.6
  56.4 0.3 fusion.63
  57.0 0.3 fusion.21
  57.4 6.6 %all_gather.14 = bf16[8,128,128]{1,2,0:T(8,128)(2,1)S(1)} all-gather(bf16[8,128,64]{1,2,0:T(8,128)(2,1)S(1)} %fusion.39), channel_id=1, replica_groups=mesh['parts'=1,'rows'=8,'branch'=2,'head'=2] {'head'}, dimensions={2}, use_global_device_ids=true | all-gather | bytes 393216 | tf_op jit(solution)/shard_map/all_gather | solution.py:153
  64.0 0.2 convolution_add_fusion.1
  64.2 17.8 %all-gather = bf16[1,32,128,32]{2,3,0,1:T(8,128)(2,1)S(1)} all-gather(bf16[1,2,128,32]{2,3,0,1:T(8,128)(2,1)S(1)} %get-tuple-element.27), channel_id=2, replica_groups=mesh['parts'=1,'rows'=8,'branch'=2,'head'=2] {'rows','branch'}, dimensions={1}, use_global_device_ids=true | all-gather | bytes 278528 | tf_op jit(solution)/shard_map/all_gather | solution.py:162
  82.2 0.7 fusion.2
  83.0 0.8 copy.51
  83.9 1.1 %fusion.13 = bf16[8,128,64]{1,2,0:T(8,128)(2,1)} fusion(f32[8,128,64]{1,2,0:T(8,128)S(1)} %convolution_add_fusion.1, bf16[8,128,1024]{1,2,0:T(8,128)(2,1)S(1)} %bitcast.130, bf16[1024,64]{0,1:T(8,128)(2,1)S(1)} %copy-done.4), kind=kOutput, calls=%fused_computation.22 | convolution fusion | flops 134348800 | bytes 2621440 | tf_op jit(solution)/shard_map/while/body/eval_jaxpr/dot_general | solution.py:177
  85.0 0.9 reshape.116
  86.0 0.7 add_convert_fusion
  (51 shorter events, 1.5 us)
Async XLA Ops:
  7.2 38.9 %copy-start = (bf16[4,256,128]{2,1,0:T(8,128)(2,1)S(1)}, bf16[4,256,128]{2,1,0:T(8,128)(2,1)}, u32[]{:S(2)}) copy-start(bf16[4,256,128]{2,1,0:T(8,128)(2,1)} %param.20) | copy-start | bytes 786436
  7.2 38.9 %copy-start.2 = (bf16[2,128,256]{2,1,0:T(8,128)(2,1)S(1)}, bf16[2,128,256]{2,1,0:T(8,128)(2,1)}, u32[]{:S(2)}) copy-start(bf16[2,128,256]{2,1,0:T(8,128)(2,1)} %param.14) | copy-start | bytes 393220
  12.3 69.8 %all-to-all-start = ((bf16[16,2,256]{2,1,0:T(2,128)(2,1)}), bf16[16,2,256]{2,1,0:T(2,128)(2,1)S(1)}, u32[]{:S(2)}, u32[]{:S(2)}) async-start(bf16[16,2,256]{2,1,0:T(2,128)(2,1)} %reshape.117), calls=%async_computation | async-start | bytes 32768 | tf_op jit(solution)/shard_map/all_to_all | solution.py:159
  19.7 65.3 %reduce-scatter.4.cloned.1.call-start = ((), (), s32[]{:S(2)}) async-start(), calls=%async_computation.2 | async-start | bytes 196608
  46.8 5.8 %copy-start.3 = (bf16[256,256]{1,0:T(8,128)(2,1)S(1)}, bf16[256,256]{1,0:T(8,128)(2,1)}, u32[]{:S(2)}) copy-start(bf16[256,256]{1,0:T(8,128)(2,1)} %param.21) | copy-start | bytes 393220
  46.9 6.3 %copy-start.7 = (bf16[512,256]{1,0:T(8,128)(2,1)S(1)}, bf16[512,256]{1,0:T(8,128)(2,1)}, u32[]{:S(2)}) copy-start(bf16[512,256]{1,0:T(8,128)(2,1)} %param.23) | copy-start | bytes 786436
  46.9 6.3 %copy-start.8 = (bf16[256,512]{1,0:T(8,128)(2,1)S(1)}, bf16[256,512]{1,0:T(8,128)(2,1)}, u32[]{:S(2)}) copy-start(bf16[256,512]{1,0:T(8,128)(2,1)} %param.22) | copy-start | bytes 786436
  47.4 7.0 %copy-start.9 = (s32[128]{0:T(128)S(1)}, s32[128]{0:T(128)}, u32[]{:S(2)}) copy-start(s32[128]{0:T(128)} %param.17) | copy-start | bytes 1540
  47.4 7.2 %copy-start.1 = (bf16[8,128,128]{2,1,0:T(8,128)(2,1)S(1)}, bf16[8,128,128]{2,1,0:T(8,128)(2,1)}, u32[]{:S(2)}) copy-start(bf16[8,128,128]{2,1,0:T(8,128)(2,1)} %param.15) | copy-start | bytes 786436
  47.4 7.2 %copy-start.5 = (bf16[4,128,64]{1,2,0:T(8,128)(2,1)S(1)}, bf16[4,128,64]{1,2,0:T(8,128)(2,1)}, u32[]{:S(2)}) copy-start(bf16[4,128,64]{1,2,0:T(8,128)(2,1)} %param.24) | copy-start | bytes 196612
  57.0 7.0 %copy-start.6 = (bf16[128,64]{0,1:T(8,128)(2,1)S(1)}, bf16[128,64]{0,1:T(8,128)(2,1)}, u32[]{:S(2)}) copy-start(bf16[128,64]{0,1:T(8,128)(2,1)} %param.25) | copy-start | bytes 49156
  82.9 0.9 copy-start.4
Sparse Core Ops, SparseCore 0:
  54.5 8.4 reduce-scatter.3
where the time goes:
time: 93.9 us; the launch traced here: 93.5 us
  blocking collectives  51.8 us (55%)
  between operations  14.4 us (15%)
  matrix products  9.08 us (10%)
  starting transfers between devices  7.45 us (8%)
  other arithmetic  5.69 us (6%)
  local copies, waits for them, and re-layouts  4.99 us (5%)
    all_gather x1, blocking collectives, local(): lax.all_gather(bias_local, ('rows', 'branch'), axis=1, tiled=True)  22.2 us
    all_gather x1, blocking collectives, local(): lax.all_gather(outer_factors[1], ('rows', 'branch'), axis=0, tiled=True)  17.8 us
    all_to_all x1, starting transfers between devices, local(): lax.all_to_all(outer_factors[0], ('rows', 'branch'), split_axis=1, concat...  7.41 us
    all_gather x1, blocking collectives, local(): lax.all_gather(pair_local, 'head', axis=2, tiled=True)  6.59 us
    all_gather x1, blocking collectives, local(): lax.all_gather(alignment_local, 'head', axis=2, tiled=True)  5.14 us
    unnamed x27, local copies, waits for them, and re-layouts  2.84 us
    reduce_sum x3, other arithmetic, layer_normalize(): spread = jnp.mean(center * center, -1, keepdims=True)  2.59 us
    reduce_sum x2, other arithmetic, layer_normalize(): center = values - jnp.mean(values, -1, keepdims=True)  2.16 us
  transfers between devices with their start and end apart: 2, of which 0 were waited for; matrix products, arithmetic and copies ran while one was open for 14% of the time, Pallas kernels for 0%

commit v1 on v0

--- a/solution.py
+++ b/solution.py
@@ -156,8 +156,14 @@
         "juf,bfn->bjun", alignment_normed, left_right_maps, preferred_element_type=jnp.float32
     )
     outer_factors = (outer_factors * mask_own[None, :, :, None]).astype(jnp.bfloat16)
-    factor_rows = lax.all_to_all(
-        outer_factors[0], ("rows", "branch"), split_axis=1, concat_axis=0, tiled=True
+    factor_rows = jnp.concatenate(
+        lax.all_to_all(
+            jnp.stack(jnp.split(outer_factors[0], lax.axis_size(("rows", "branch")), axis=1)),
+            ("rows", "branch"),
+            0,
+            0,
+        ),
+        axis=0,
     )
     col_factors = lax.all_gather(outer_factors[1], ("rows", "branch"), axis=0, tiled=True)
     mask_rows = lax.dynamic_slice_in_dim(mask_full, row_start, residue_shard_count, 1)

time: 93.9 us -> 93.3 us (level)
  local copies, waits for them, and re-layouts: 4.99 us -> 6.46 us
  matrix products: 9.08 us -> 8.1 us
  other arithmetic: 5.69 us -> 4.73 us
    another operation x0 -> x18, local copies, waits for them, and re-layouts: none -> 1.48 us  [local(): jnp.stack(jnp.split(outer_factors[0], lax.axis_size(('rows', 'branch')),...]
    dot_general x1, matrix products: 1.43 us -> 0.45 us  [local(): jnp.einsum('tue,el->ltu', pair_normed, bias_matrix, preferred_element_typ...]
    reduce_sum x3, other arithmetic: 2.59 us -> 1.63 us  [layer_normalize(): spread = jnp.mean(center * center, -1, keepdims=True)]
    unnamed x27 -> x46, local copies, waits for them, and re-layouts: 2.84 us -> 2.97 us
  transfers between devices with their start and end apart: 2 -> 2, of which waited for: 0 -> 0; matrix products, arithmetic and copies ran while one was open for 14% -> 12% of each run, Pallas kernels for 0% -> 0%
where the time goes in v1:
time: 93.3 us; the launch traced here: 92.9 us
  blocking collectives  51.7 us (55%)
  between operations  14.5 us (16%)
  matrix products  8.1 us (9%)
  starting transfers between devices  7.45 us (8%)
  local copies, waits for them, and re-layouts  6.46 us (7%)
  other arithmetic  4.73 us (5%)
    all_gather x1, blocking collectives, local(): lax.all_gather(bias_local, ('rows', 'branch'), axis=1, tiled=True)  22.2 us
    all_gather x1, blocking collectives, local(): lax.all_gather(outer_factors[1], ('rows', 'branch'), axis=0, tiled=True)  17.8 us
    all_to_all x1, starting transfers between devices, local(): lax.all_to_all(jnp.stack(jnp.split(outer_factors[0], lax.axis_size(('rows...  7.41 us
    all_gather x1, blocking collectives, local(): lax.all_gather(pair_local, 'head', axis=2, tiled=True)  6.59 us
    all_gather x1, blocking collectives, local(): lax.all_gather(alignment_local, 'head', axis=2, tiled=True)  5.01 us
    unnamed x46, local copies, waits for them, and re-layouts  2.97 us
    reduce_sum x2, other arithmetic, layer_normalize(): center = values - jnp.mean(values, -1, keepdims=True)  2.16 us
  transfers between devices with their start and end apart: 2, of which 0 were waited for; matrix products, arithmetic and copies ran while one was open for 12% of the time, Pallas kernels for 0%

profile of v1, /device:TPU:0, one launch (start us, length us, event | category | flops | bytes accessed | tf_op | source)
XLA Modules:
  0.0 92.9 jit_solution(5612878842681667742)
XLA Ops:
  7.2 1.1 %convert_reduce_fusion.1 = f32[2,128]{1,0:T(2,128)S(1)} fusion(bf16[2,128,256]{2,1,0:T(8,128)(2,1)} %param.14), kind=kLoop, calls=%fused_computation.38 | loop fusion | flops 130816 | bytes 132096 | tf_op jit(solution)/shard_map/reduce_sum | solution.py:12
  8.3 1.1 %fusion.24 = f32[2,128]{1,0:T(2,128)S(1)} fusion(bf16[2,128,256]{2,1,0:T(8,128)(2,1)} %param.14, f32[2,128]{1,0:T(2,128)S(1)} %broadcast_multiply_fusion.2), kind=kLoop, calls=%fused_computation.41 | loop fusion | flops 261888 | bytes 133120 | tf_op jit(solution)/shard_map/reduce_sum | solution.py:13
  9.4 0.8 slice_bitcast_fusion.18
  10.3 1.2 %fusion.16 = bf16[2,2,128,32]{2,3,0,1:T(8,128)(2,1)S(1)} fusion(bf16[2,128,256]{2,1,0:T(8,128)(2,1)} %param.14, f32[2,128]{1,0:T(2,128)S(1)} %add_rsqrt_fusion.2, f32[2,128]{1,0:T(2,128)S(1)} %broadcast_multiply_fusion.2, bf16[2,256,32]{1,2,0:T(8,128)(2,1)} %param.26, f32[2,128]{1,0:T(2,128)S(1)} %get-tuple-element.44), kind=kOutput, calls=%fused_computation.26 | convolution fusion | flops 8683520 | bytes 199680 | tf_op jit(solution)/shard_map/juf,bfn->bjun/dot_general | solution.py:155
  13.1 0.7 reshape.121
  13.9 7.4 %all-to-all-start = ((bf16[16,2,256]{2,1,0:T(2,128)(2,1)}), bf16[16,2,256]{2,1,0:T(2,128)(2,1)S(1)}, u32[]{:S(2)}, u32[]{:S(2)}) async-start(bf16[16,2,256]{2,1,0:T(2,128)(2,1)} %reshape.121), calls=%async_computation | async-start | bytes 32768 | tf_op jit(solution)/shard_map/all_to_all | solution.py:160
  21.3 1.1 %convert_reduce_fusion = f32[8,128]{1,0:T(8,128)S(1)} fusion(bf16[8,128,128]{2,1,0:T(8,128)(2,1)} %param.15), kind=kLoop, calls=%fused_computation.30 | loop fusion | flops 261120 | bytes 266240 | tf_op jit(solution)/shard_map/reduce_sum | solution.py:12
  22.4 0.4 fusion.19
  22.8 0.5 convolution_convert_fusion
  23.3 22.2 %all_gather.12 = bf16[6,128,128]{2,1,0:T(8,128)(2,1)S(1)} all-gather(bf16[6,8,128]{2,1,0:T(8,128)(2,1)S(1)} %copy.65), channel_id=1, replica_groups=mesh['parts'=1,'rows'=8,'branch'=2,'head'=2] {'rows','branch'}, dimensions={1}, use_global_device_ids=true | all-gather | bytes 208896 | tf_op jit(solution)/shard_map/all_gather | solution.py:87
  45.7 0.4 fusion.78
  46.1 0.4 fusion.79
  46.5 0.3 fusion.10
  46.8 0.2 fusion.40
  47.1 5.0 %all_gather.13 = bf16[2,128,256]{1,2,0:T(8,128)(2,1)S(1)} all-gather(bf16[2,128,128]{1,2,0:T(8,128)(2,1)S(1)} %fusion.55), channel_id=1, replica_groups=mesh['parts'=1,'rows'=8,'branch'=2,'head'=2] {'head'}, dimensions={2}, use_global_device_ids=true | all-gather | bytes 196608 | tf_op jit(solution)/shard_map/all_gather | solution.py:152
  52.1 0.3 fusion.80
  52.5 0.2 multiply_reduce_fusion
  52.7 0.4 fusion.14
  53.2 0.7 copy.114
  54.1 0.9 fusion.81
  55.0 0.6 fusion.82
  55.6 0.4 fusion.6
  55.9 0.3 fusion.63
  56.5 0.3 fusion.21
  56.9 6.6 %all_gather.14 = bf16[8,128,128]{1,2,0:T(8,128)(2,1)S(1)} all-gather(bf16[8,128,64]{1,2,0:T(8,128)(2,1)S(1)} %fusion.39), channel_id=1, replica_groups=mesh['parts'=1,'rows'=8,'branch'=2,'head'=2] {'head'}, dimensions={2}, use_global_device_ids=true | all-gather | bytes 393216 | tf_op jit(solution)/shard_map/all_gather | solution.py:153
  63.5 0.2 convolution_add_fusion.1
  63.7 17.8 %all-gather = bf16[1,32,128,32]{2,3,0,1:T(8,128)(2,1)S(1)} all-gather(bf16[1,2,128,32]{2,3,0,1:T(8,128)(2,1)S(1)} %get-tuple-element.27), channel_id=2, replica_groups=mesh['parts'=1,'rows'=8,'branch'=2,'head'=2] {'rows','branch'}, dimensions={1}, use_global_device_ids=true | all-gather | bytes 278528 | tf_op jit(solution)/shard_map/all_gather | solution.py:168
  81.7 0.7 fusion.2
  82.4 0.8 copy.90
  83.3 1.1 %fusion.13 = bf16[8,128,64]{1,2,0:T(8,128)(2,1)} fusion(f32[8,128,64]{1,2,0:T(8,128)S(1)} %convolution_add_fusion.1, bf16[8,128,1024]{1,2,0:T(8,128)(2,1)S(1)} %bitcast.155, bf16[1024,64]{0,1:T(8,128)(2,1)S(1)} %copy-done.4), kind=kOutput, calls=%fused_computation.22 | convolution fusion | flops 134348800 | bytes 2621440 | tf_op jit(solution)/shard_map/while/body/eval_jaxpr/dot_general | solution.py:183
  84.4 0.9 reshape.120
  85.4 0.7 add_convert_fusion
  (85 shorter events, 3.0 us)
Async XLA Ops:
  7.2 38.5 %copy-start = (bf16[4,256,128]{2,1,0:T(8,128)(2,1)S(1)}, bf16[4,256,128]{2,1,0:T(8,128)(2,1)}, u32[]{:S(2)}) copy-start(bf16[4,256,128]{2,1,0:T(8,128)(2,1)} %param.20) | copy-start | bytes 786436
  7.2 38.5 %copy-start.2 = (bf16[2,128,256]{2,1,0:T(8,128)(2,1)S(1)}, bf16[2,128,256]{2,1,0:T(8,128)(2,1)}, u32[]{:S(2)}) copy-start(bf16[2,128,256]{2,1,0:T(8,128)(2,1)} %param.14) | copy-start | bytes 393220
  7.2 15.2 %copy-start.1 = (bf16[8,128,128]{2,1,0:T(8,128)(2,1)S(1)}, bf16[8,128,128]{2,1,0:T(8,128)(2,1)}, u32[]{:S(2)}) copy-start(bf16[8,128,128]{2,1,0:T(8,128)(2,1)} %param.15) | copy-start | bytes 786436
  7.2 15.6 %copy-start.10 = (bf16[128,2]{0,1:T(2,128)(2,1)S(1)}, bf16[128,2]{0,1:T(2,128)(2,1)}, u32[]{:S(2)}) copy-start(bf16[128,2]{0,1:T(2,128)(2,1)} %param.19) | copy-start | bytes 1540
  7.2 15.6 %copy-start.9 = (bf16[128,4]{0,1:T(4,128)(2,1)S(1)}, bf16[128,4]{0,1:T(4,128)(2,1)}, u32[]{:S(2)}) copy-start(bf16[128,4]{0,1:T(4,128)(2,1)} %param.18) | copy-start | bytes 3076
  13.9 67.7 %all-to-all-start = ((bf16[16,2,256]{2,1,0:T(2,128)(2,1)}), bf16[16,2,256]{2,1,0:T(2,128)(2,1)S(1)}, u32[]{:S(2)}, u32[]{:S(2)}) async-start(bf16[16,2,256]{2,1,0:T(2,128)(2,1)} %reshape.121), calls=%async_computation | async-start | bytes 32768 | tf_op jit(solution)/shard_map/all_to_all | solution.py:160
  21.3 63.2 %reduce-scatter.4.cloned.1.call-start = ((), (), s32[]{:S(2)}) async-start(), calls=%async_computation.2 | async-start | bytes 196608
  46.5 5.6 %copy-start.3 = (bf16[256,256]{1,0:T(8,128)(2,1)S(1)}, bf16[256,256]{1,0:T(8,128)(2,1)}, u32[]{:S(2)}) copy-start(bf16[256,256]{1,0:T(8,128)(2,1)} %param.21) | copy-start | bytes 393220
  46.5 6.1 %copy-start.7 = (bf16[512,256]{1,0:T(8,128)(2,1)S(1)}, bf16[512,256]{1,0:T(8,128)(2,1)}, u32[]{:S(2)}) copy-start(bf16[512,256]{1,0:T(8,128)(2,1)} %param.23) | copy-start | bytes 786436
  46.5 6.1 %copy-start.8 = (bf16[256,512]{1,0:T(8,128)(2,1)S(1)}, bf16[256,512]{1,0:T(8,128)(2,1)}, u32[]{:S(2)}) copy-start(bf16[256,512]{1,0:T(8,128)(2,1)} %param.22) | copy-start | bytes 786436
  47.1 6.9 %copy-start.11 = (s32[128]{0:T(128)S(1)}, s32[128]{0:T(128)}, u32[]{:S(2)}) copy-start(s32[128]{0:T(128)} %param.17) | copy-start | bytes 1540
  47.1 7.0 %copy-start.5 = (bf16[4,128,64]{1,2,0:T(8,128)(2,1)S(1)}, bf16[4,128,64]{1,2,0:T(8,128)(2,1)}, u32[]{:S(2)}) copy-start(bf16[4,128,64]{1,2,0:T(8,128)(2,1)} %param.24) | copy-start | bytes 196612
  56.5 7.0 %copy-start.6 = (bf16[128,64]{0,1:T(8,128)(2,1)S(1)}, bf16[128,64]{0,1:T(8,128)(2,1)}, u32[]{:S(2)}) copy-start(bf16[128,64]{0,1:T(8,128)(2,1)} %param.25) | copy-start | bytes 49156
  82.4 0.9 copy-start.4
Sparse Core Ops, SparseCore 0:
  54.0 8.4 reduce-scatter.3
